TPU v7x, 32 devices: a whole 2x2x4 slice. The times are simulated.
32 devices in a mesh: grp: 2 (over y), kx: 4 (over z), ky: 2 (over x), ex: 2 (over core).
Axes of the slice: x: 2, y: 2, z: 4, core: 2. Of those that a mesh axis runs over, the one named last changes fastest.
Arguments:
- basis: bfloat16 [1024, 4, 4, 1024], P(None, 'kx', ('ky', 'ex')), may hold values from -6 to 6
- ritz: bfloat16 [1024, 192], P('kx'), may hold values from -0.1875 to 0.1875
- phonon_g: bfloat16 [6, 4, 4, 16384], P(None, 'kx', ('ky', 'ex')), may hold values from -6 to 6
- band_index: int32 [8], replicated, may hold values from 0 to 15, as said below
- qshift: int32 [6], P('grp'), parts along dimension 0, may hold values from 0 to 63, as said below
Outputs:
- coupling: float32 [12, 192, 192], P('grp', 'kx', ('ky', 'ex')), parts along dimension 0
There are 2 independent parts, one for each index of `grp`. A program takes and returns all parts, laid end to end along the dimension named above; an argument that names none is the same for every part. Nothing has to cross between parts.
Inputs may be any that keep to these rules, and one draw needn't show every extreme that they name: `qshift`: component 0 lies in 1 to 3, component 1 in 0 to 63, component 2 in 1 to 3; the same for all k-points of a part; in the first part component 1 is 63. `band_index`: the first 4 entries are distinct and below 8, the last 4 entries are distinct and at least 8.
All inputs are finite; a program needn't handle non-finite values.
Results may differ from a plain program's by a relative error of at most 0.0049.
Values may be sent and summed in bfloat16 or wider, within the bound.
A program may use at most 64 MiB of HBM per device.

v0:
```python
import math

import jax
import jax.numpy as jnp
from jax import lax
from jax.sharding import PartitionSpec as P

NV = 4
NC = 4
ALLB = 16


def passed_along(value, axis, steps):
    count = lax.axis_size(axis)
    pairs = [(source, (source + steps) % count) for source in range(count)]
    return lax.ppermute(value, axis, pairs)


def band_mix(amplitude, cond_mode, val_mode):
    cond_part = jnp.sum(cond_mode[None, None] * amplitude[:, :, None], axis=3)
    val_part = jnp.sum(val_mode[None, :, :, None] * amplitude[:, :, None], axis=1)
    return cond_part - val_part


def band_tables(phonon_g, band_index, count_val):
    all_bands = ALLB
    labels = jnp.arange(all_bands, dtype=jnp.int32)
    selector = (band_index[:, None] == labels[None, :]).astype(jnp.bfloat16)
    val_select = selector[:count_val]
    cond_select = selector[count_val:]
    coupling_table = phonon_g.reshape(phonon_g.shape[0], all_bands, all_bands, -1)
    val_table = jnp.einsum(
        "ia,uabk,jb->uijk",
        val_select,
        coupling_table,
        val_select,
        preferred_element_type=jnp.float32,
    )
    cond_table = jnp.einsum(
        "ia,uabk,jb->uijk",
        cond_select,
        coupling_table,
        cond_select,
        preferred_element_type=jnp.float32,
    )
    return (val_table, cond_table)


def shards(basis, ritz, phonon_g, band_index, qshift):
    count_exc = ritz.shape[1]
    count_val = NV
    count_cond = NC
    width_y = basis.shape[3] // (count_val * count_cond)
    basis_flat = basis.reshape(basis.shape[0], -1)
    excitons = lax.dot_general(
        lax.all_gather(ritz, "kx", axis=0, tiled=True),
        basis_flat,
        (((0,), (0,)), ((), ())),
        preferred_element_type=jnp.float32,
    ).astype(jnp.bfloat16)
    planes_x = lax.axis_size("kx")
    planes_z = lax.axis_size(("ky", "ex"))
    carried = excitons
    for bit_place in range(planes_x.bit_length() - 1):
        arrived = passed_along(carried, "kx", -(1 << bit_place))
        carried = jnp.where(qshift[0] // (1 << bit_place) % 2 == 1, arrived, carried)
    for bit_place in range(planes_z.bit_length() - 1):
        arrived = passed_along(carried, ("ky", "ex"), -(1 << bit_place))
        carried = jnp.where(qshift[2] // (1 << bit_place) % 2 == 1, arrived, carried)
    shifted = jnp.roll(
        carried.reshape(count_exc, count_val, count_cond, width_y), -qshift[1], axis=3
    )
    shifted_rows = shifted.reshape(count_exc, -1)
    amplitude = excitons.reshape(count_exc, count_val, count_cond, width_y).astype(jnp.float32)
    val_table, cond_table = band_tables(phonon_g, band_index, count_val)
    blocks = []
    for mode_index in range(phonon_g.shape[0]):
        mixed_band = band_mix(amplitude, cond_table[mode_index], val_table[mode_index]).astype(
            jnp.bfloat16
        )
        blocks.append(
            lax.dot_general(
                shifted_rows,
                mixed_band.reshape(count_exc, -1),
                (((1,), (1,)), ((), ())),
                preferred_element_type=jnp.float32,
            )
        )
    partial_value = jnp.stack(blocks)
    norm_factor = 1.0 / math.sqrt(count_val * count_cond * width_y * planes_x * planes_z)
    own_cols = lax.psum_scatter(partial_value, ("ky", "ex"), scatter_dimension=2, tiled=True)
    coupling = lax.psum_scatter(own_cols, "kx", scatter_dimension=1, tiled=True)
    return coupling * norm_factor


def solution(mesh):
    placed = (
        P(None, "kx", ("ky", "ex"), None),
        P("kx", None),
        P(None, "kx", ("ky", "ex"), None),
        P(),
        P("grp"),
    )
    return jax.shard_map(
        shards, mesh=mesh, in_specs=placed, out_specs=P("grp", "kx", ("ky", "ex")), check_vma=False
    )
```

profile of v0, /device:TPU:1, one launch (start us, length us, event | category | flops | bytes accessed | tf_op | source)
XLA Modules:
  0.0 150.4 jit_solution(14850392606737595001)
XLA Ops:
  6.5 14.2 %all_gather.3 = bf16[1024,192]{0,1:T(8,128)(2,1)S(1)} all-gather(bf16[256,192]{0,1:T(8,128)(2,1)} %param.6), channel_id=1, replica_groups=mesh['grp'=2,'kx'=4,'ky'=2,'ex'=2] {'kx'}, dimensions={0}, use_global_device_ids=true | all-gather | bytes 491520 | tf_op jit(solution)/shard_map/all_gather | solution.py:56
  20.8 1.3 fusion.2
  22.1 1.9 %collective-permute-start = (bf16[192,1024]{1,0:T(8,128)(2,1)}, bf16[192,1024]{1,0:T(8,128)(2,1)}, u32[]{:S(2)}, u32[]{:S(2)}) collective-permute-start(bf16[192,1024]{1,0:T(8,128)(2,1)} %fusion.2), channel_id=1, source_target_pairs={{0,12},{4,0},{8,4},{12,8},{1,13},{5,1},{9,5},{13,9},{2,14},{6,2},{... | collective-permute-start | bytes 1179656 | tf_op jit(solution)/shard_map/ppermute | solution.py:16
  24.0 1.4 fusion.24
  31.6 1.2 copy.40
  32.8 1.3 reshape.39
  34.3 0.2 convolution_bitcast_fusion.7
  34.5 1.1 broadcast_select_fusion
  35.6 0.1 convolution_bitcast_fusion.9
  35.7 0.2 convolution_bitcast_fusion.6
  35.9 19.3 %collective-permute-done.1 = bf16[192,1024]{1,0:T(8,128)(2,1)S(1)} collective-permute-done((bf16[192,1024]{1,0:T(8,128)(2,1)S(1)}, bf16[192,1024]{1,0:T(8,128)(2,1)S(1)}, u32[]{:S(2)}, u32[]{:S(2)}) %collective-permute-start.1) | collective-permute-done | bytes 393248 | tf_op jit(solution)/shard_map/ppermute | solution.py:16
  55.2 0.5 collective-permute-start.2
  55.8 0.1 convolution_bitcast_fusion.8
  55.9 6.6 %collective-permute-done.2 = bf16[192,1024]{1,0:T(8,128)(2,1)S(1)} collective-permute-done((bf16[192,1024]{1,0:T(8,128)(2,1)S(1)}, bf16[192,1024]{1,0:T(8,128)(2,1)S(1)}, u32[]{:S(2)}, u32[]{:S(2)}) %collective-permute-start.2) | collective-permute-done | bytes 393248 | tf_op jit(solution)/shard_map/ppermute | solution.py:16
  62.5 1.3 collective-permute-start.3
  63.8 11.4 %multiply_reduce_fusion = (f32[192,4,4,64]{0,3,2,1:T(8,128)}, f32[192,4,4,64]{0,3,2,1:T(8,128)}, f32[192,4,4,64]{0,3,2,1:T(8,128)}, f32[192,4,4,64]{0,3,2,1:T(8,...) fusion(f32[4,4,64]{2,1,0:T(4,128)S(1)} %get-tuple-element.24, ...), kind=kLoop, calls=%fused_computation | loop fusion | flops 16515072 | bytes 10272768 | tf_op jit(solution)/shard_map/reduce_sum | solution.py:21
  75.3 1.0 copy.37
  76.3 1.6 %fusion.11 = bf16[192,4,4,64]{0,3,2,1:T(8,128)(2,1)S(1)} fusion(s32[]{:T(128)S(6)} %select_n.81, bf16[192,4,4,64]{0,3,2,1:T(8,128)(2,1)} %bitcast.119), kind=kLoop, calls=%fused_computation.39 | loop fusion | flops 786432 | bytes 786436 | tf_op jit(solution)/shard_map/jit(_roll_dynamic)/concatenate | solution.py:70
  77.9 2.7 %fusion.10 = f32[6,192,192]{2,1,0:T(8,128)} fusion(bf16[192,4,4,64]{0,3,2,1:T(8,128)(2,1)S(1)} %fusion.11, f32[192,4,4,64]{0,3,2,1:T(8,128)} %get-tuple-element.16, f32[192,4,4,64]{0,3,2,1:T(8,128)} %get-tuple-element.6), kind=kOutput, calls=%fused_computation.26 | convolution fusion | flops 75890688 | bytes 2162688 | tf_op jit(solution)/shard_map/dot_general | solution.py:82
  80.6 1.0 fusion.9
  81.6 1.0 fusion.8
  82.6 1.0 fusion.7
  83.6 1.0 fusion.6
  84.6 1.0 fusion.5
  85.6 3.2 %copy.43 = f32[6,192,192]{1,0,2:T(8,128)} copy(f32[6,192,192]{2,1,0:T(8,128)} %fusion.5) | data formatting | bytes 1769472 | tf_op jit(solution)/shard_map/stack | solution.py:89
  88.9 25.3 %reduce-scatter.5.cloned.1.call-done = f32[6,192,48]{1,0,2:T(8,128)} async-done(((f32[6,192,192]{1,0,2:T(8,128)}), f32[6,192,48]{1,0,2:T(8,128)}) %reduce-scatter.5.cloned.1.call-update) | async-done | bytes 221200 | tf_op jit(solution)/shard_map/reduce_scatter | solution.py:91
  114.2 4.0 %copy.53 = f32[6,192,48]{0,2,1:T(8,128)} copy(f32[6,192,48]{1,0,2:T(8,128)} %reduce-scatter.5.cloned.1.call-done) | data formatting | bytes 442368
  118.2 4.3 %reshape.49 = f32[192,288]{1,0:T(8,128)} reshape(f32[192,48,6]{2,1,0:T(8,128)} %bitcast.116) | data formatting | bytes 442368
  122.5 18.4 %reduce-scatter.7.cloned.1.call-done = f32[48,288]{1,0:T(8,128)} async-done(((f32[192,288]{1,0:T(8,128)}), f32[48,288]{1,0:T(8,128)}) %reduce-scatter.7.cloned.1.call-update) | async-done | bytes 55312
  140.9 1.5 reshape.50
  142.4 0.4 copy.44
  142.8 0.7 broadcast_multiply_fusion
  (36 shorter events, 0.4 us)
Async XLA Ops:
  6.5 14.2 %copy-start = (bf16[1024,1,1,1024]{3,0,2,1:T(8,128)(2,1)S(1)}, bf16[1024,1,1,1024]{3,0,2,1:T(8,128)(2,1)}, u32[]{:S(2)}) copy-start(bf16[1024,1,1,1024]{3,0,2,1:T(8,128)(2,1)} %param.5) | copy-start | bytes 6291460
  6.5 27.6 %copy-start.11 = (s32[8]{0:T(128)S(1)}, s32[8]{0:T(128)}, u32[]{:S(2)}) copy-start(s32[8]{0:T(128)} %param.8) | copy-start | bytes 100
  6.5 107.7 %reduce-scatter.5.cloned.1.call-start = ((), (), s32[]{:S(2)}) async-start(), calls=%async_computation.2 | async-start | bytes 1966080 | tf_op jit(solution)/shard_map/reduce_scatter | solution.py:91
  22.1 12.4 %collective-permute-start = (bf16[192,1024]{1,0:T(8,128)(2,1)}, bf16[192,1024]{1,0:T(8,128)(2,1)}, u32[]{:S(2)}, u32[]{:S(2)}) collective-permute-start(bf16[192,1024]{1,0:T(8,128)(2,1)} %fusion.2), channel_id=1, source_target_pairs={{0,12},{4,0},{8,4},{12,8},{1,13},{5,1},{9,5},{13,9},{2,14},{6,2},{... | collective-permute-start | bytes 1179656 | tf_op jit(solution)/shard_map/ppermute | solution.py:16
  35.5 19.7 %collective-permute-start.1 = (bf16[192,1024]{1,0:T(8,128)(2,1)S(1)}, bf16[192,1024]{1,0:T(8,128)(2,1)S(1)}, u32[]{:S(2)}, u32[]{:S(2)}) collective-permute-start(bf16[192,1024]{1,0:T(8,128)(2,1)S(1)} %broadcast_select_fusion), channel_id=1, source_target_pairs={{0,8},{4,12},{8,0},{12,4},{1,9},{5,13},{9,1},{13,5},{2,10},{6,14},... | collective-permute-start | bytes 1179656 | tf_op jit(solution)/shard_map/ppermute | solution.py:16
  55.2 7.3 %collective-permute-start.2 = (bf16[192,1024]{1,0:T(8,128)(2,1)S(1)}, bf16[192,1024]{1,0:T(8,128)(2,1)S(1)}, u32[]{:S(2)}, u32[]{:S(2)}) collective-permute-start(bf16[192,1024]{1,0:T(8,128)(2,1)S(1)} %broadcast_select_fusion.1), channel_id=1, source_target_pairs={{0,3},{1,0},{2,1},{3,2},{4,7},{5,4},{6,5},{7,6},{8,11},{9,8},{10,9... | collective-permute-start | bytes 1179656 | tf_op jit(solution)/shard_map/ppermute | solution.py:16
  62.5 12.7 %collective-permute-start.3 = (bf16[192,1024]{1,0:T(8,128)(2,1)S(1)}, bf16[192,1024]{1,0:T(8,128)(2,1)S(1)}, u32[]{:S(2)}, u32[]{:S(2)}) collective-permute-start(bf16[192,1024]{1,0:T(8,128)(2,1)S(1)} %broadcast_select_fusion.2), channel_id=1, source_target_pairs={{0,2},{1,3},{2,0},{3,1},{4,6},{5,7},{6,4},{7,5},{8,10},{9,11},{10,... | collective-permute-start | bytes 1179656 | tf_op jit(solution)/shard_map/ppermute | solution.py:16
  75.2 6.4 %copy-start.7 = (f32[192,4,4,64]{0,3,2,1:T(8,128)S(1)}, f32[192,4,4,64]{0,3,2,1:T(8,128)}, u32[]{:S(2)}) copy-start(f32[192,4,4,64]{0,3,2,1:T(8,128)} %get-tuple-element.9) | copy-start | bytes 2359300
  76.2 4.3 %copy-start.9 = (f32[192,4,4,64]{0,3,2,1:T(8,128)S(1)}, f32[192,4,4,64]{0,3,2,1:T(8,128)}, u32[]{:S(2)}) copy-start(f32[192,4,4,64]{0,3,2,1:T(8,128)} %get-tuple-element.7) | copy-start | bytes 2359300
  76.2 4.3 %copy-start.10 = (f32[192,4,4,64]{0,3,2,1:T(8,128)S(1)}, f32[192,4,4,64]{0,3,2,1:T(8,128)}, u32[]{:S(2)}) copy-start(f32[192,4,4,64]{0,3,2,1:T(8,128)} %get-tuple-element.8) | copy-start | bytes 2359300
  76.3 5.4 %copy-start.8 = (f32[192,4,4,64]{0,3,2,1:T(8,128)S(1)}, f32[192,4,4,64]{0,3,2,1:T(8,128)}, u32[]{:S(2)}) copy-start(f32[192,4,4,64]{0,3,2,1:T(8,128)} %get-tuple-element.10) | copy-start | bytes 2359300
  77.9 4.7 %copy-start.5 = (f32[192,4,4,64]{0,3,2,1:T(8,128)S(1)}, f32[192,4,4,64]{0,3,2,1:T(8,128)}, u32[]{:S(2)}) copy-start(f32[192,4,4,64]{0,3,2,1:T(8,128)} %get-tuple-element.11) | copy-start | bytes 2359300
  77.9 4.7 %copy-start.6 = (f32[192,4,4,64]{0,3,2,1:T(8,128)S(1)}, f32[192,4,4,64]{0,3,2,1:T(8,128)}, u32[]{:S(2)}) copy-start(f32[192,4,4,64]{0,3,2,1:T(8,128)} %get-tuple-element.12) | copy-start | bytes 2359300
  80.6 3.0 %copy-start.3 = (f32[192,4,4,64]{0,3,2,1:T(8,128)S(1)}, f32[192,4,4,64]{0,3,2,1:T(8,128)}, u32[]{:S(2)}) copy-start(f32[192,4,4,64]{0,3,2,1:T(8,128)} %get-tuple-element.13) | copy-start | bytes 2359300
  80.6 3.0 %copy-start.4 = (f32[192,4,4,64]{0,3,2,1:T(8,128)S(1)}, f32[192,4,4,64]{0,3,2,1:T(8,128)}, u32[]{:S(2)}) copy-start(f32[192,4,4,64]{0,3,2,1:T(8,128)} %get-tuple-element.14) | copy-start | bytes 2359300
  81.6 3.0 %copy-start.1 = (f32[192,4,4,64]{0,3,2,1:T(8,128)S(1)}, f32[192,4,4,64]{0,3,2,1:T(8,128)}, u32[]{:S(2)}) copy-start(f32[192,4,4,64]{0,3,2,1:T(8,128)} %get-tuple-element.5) | copy-start | bytes 2359300
  81.6 3.0 %copy-start.2 = (f32[192,4,4,64]{0,3,2,1:T(8,128)S(1)}, f32[192,4,4,64]{0,3,2,1:T(8,128)}, u32[]{:S(2)}) copy-start(f32[192,4,4,64]{0,3,2,1:T(8,128)} %get-tuple-element.15) | copy-start | bytes 2359300
  88.8 52.1 %reduce-scatter.7.cloned.1.call-start = ((), (), s32[]{:S(2)}) async-start(), calls=%async_computation.3 | async-start | bytes 368640
Sparse Core Ops, SparseCore 0:
  88.9 25.2 reduce-scatter.4
  122.6 18.2 reduce-scatter.6
where the time goes:
time: 153 us; the launch traced here: 150 us
  waiting for transfers between devices  69.6 us (45%)
  between operations  19.7 us (13%)
  local copies, waits for them, and re-layouts  18.4 us (12%)
  other arithmetic  15 us (10%)
  blocking collectives  14.2 us (9%)
  matrix products  9.65 us (6%)
  starting transfers between devices  3.88 us (3%)
    ppermute x4, waiting for transfers between devices, passed_along(): return lax.ppermute(value, axis, pairs)  25.8 us
    reduce_scatter x1, waiting for transfers between devices, shards(): lax.psum_scatter(partial_value, ('ky', 'ex'), scatter_dimension=2, tiled=...  25.3 us
    unnamed x3, waiting for transfers between devices  18.4 us
    all_gather x1, blocking collectives, shards(): lax.all_gather(ritz, 'kx', axis=0, tiled=True)  14.2 us
    reduce_sum x1, other arithmetic, band_mix(): jnp.sum(val_mode[None, :, :, None] * amplitude[:, :, None], axis=1)  11.4 us
    unnamed x27, local copies, waits for them, and re-layouts  9.81 us
    dot_general x6, matrix products, shards(): lax.dot_general(shifted_rows, mixed_band.reshape(count_exc, -1), (((1,),...  7.68 us
    ppermute x4, starting transfers between devices, passed_along(): return lax.ppermute(value, axis, pairs)  3.84 us
  transfers between devices with their start and end apart: 6, of which 4 were waited for; matrix products, arithmetic and copies ran while one was open for 11% of the time, Pallas kernels for 0%

commit v1 on v0

--- a/solution.py
+++ b/solution.py
@@ -1,13 +1,18 @@
+import functools
 import math
 
 import jax
 import jax.numpy as jnp
 from jax import lax
+from jax.experimental import pallas as pl
+from jax.experimental.pallas import tpu as pltpu
 from jax.sharding import PartitionSpec as P
 
 NV = 4
 NC = 4
 ALLB = 16
+LANES = 128
+MESH = pl.DeviceIdType.MESH
 
 
 def passed_along(value, axis, steps):
@@ -46,7 +51,7 @@
     return (val_table, cond_table)
 
 
-def shards(basis, ritz, phonon_g, band_index, qshift):
+def by_collectives(basis, ritz, phonon_g, band_index, qshift):
     count_exc = ritz.shape[1]
     count_val = NV
     count_cond = NC
@@ -93,6 +98,360 @@
     return coupling * norm_factor
 
 
+def tables(planes_x, planes_z, band_ref, q_ref, phonon_ref, coefs, permute, wanted):
+    modes = phonon_ref.shape[0]
+    halves = NC // 2
+    lane = lax.broadcasted_iota(jnp.int32, (modes, LANES), 1)
+    low = lane < LANES // 2
+
+    def on_both(left, right):
+        row = band_ref[left] * ALLB + band_ref[right]
+        at = pl.multiple_of((row // 2) * LANES, LANES)
+        tile = phonon_ref[:, pl.ds(at, LANES)].astype(jnp.float32)
+        other = pltpu.roll(tile, LANES // 2, 1)
+        odd = row % 2
+        return jnp.where(low == (odd == 0), tile, other)
+
+    for w in range(NV):
+        for v in range(NV):
+            coefs[w * NV + v, :modes, :] = on_both(w, v)
+    for ch in range(halves):
+        for dh in range(halves):
+            for off in range(2):
+                lower = on_both(NV + 2 * ch, NV + 2 * dh + off)
+                upper = on_both(NV + 2 * ch + 1, NV + 2 * dh + 1 - off)
+                place = NV * NV + (ch * halves + dh) * 2 + off
+                coefs[place, :modes, :] = jnp.where(low, lower, upper)
+
+    come = lax.broadcasted_iota(jnp.int32, (LANES, LANES), 0)
+    goes = lax.broadcasted_iota(jnp.int32, (LANES, LANES), 1)
+    width = LANES // 2
+    source = (goes // width) * width + (goes % width + q_ref[1]) % width
+    permute[...] = (come == source).astype(jnp.bfloat16)
+
+    for target in range(planes_x * planes_z):
+        x = (target // planes_z + q_ref[0]) % planes_x
+        z = (target % planes_z + q_ref[2]) % planes_z
+        wanted[target : target + 1, :] = jnp.full((1, LANES), x * planes_z + z, jnp.int32)
+
+
+def whole_step(
+    planes_x, planes_z, norm_factor,
+    coefs, permute, wanted, ritz_ref, basis_ref, out_ref,
+    gathered, total, exc_ref, slices, first, second_out, second_in,
+    mixed, shifted, sum_out, sum_in, turned, last_out, last_in,
+    ritz_send, ritz_recv, fwd_send, fwd_recv,
+    one_send, one_recv, two_send, two_recv, a_send, a_recv, b_send, b_recv,
+):
+    planes = planes_x * planes_z
+    grp = lax.axis_index("grp")
+    kx = lax.axis_index("kx")
+    ky = lax.axis_index("ky")
+    ex = lax.axis_index("ex")
+    kz = ky * 2 + ex
+    me = kx * planes_z + kz
+    modes = out_ref.shape[0]
+    count_exc, depth = ritz_ref.shape
+    half = depth // 2
+    tiles = exc_ref.shape[1] // LANES
+    halves = NC // 2
+
+    def device(plane):
+        z = plane % planes_z
+        return (grp, plane // planes_z, z // 2, z % 2)
+
+    barrier = pltpu.get_barrier_semaphore()
+    for step in range(1, planes):
+        pl.semaphore_signal(
+            barrier, inc=1, device_id=device((me + step) % planes), device_id_type=MESH
+        )
+    gathered[kx, 0] = ritz_ref[:, :half]
+    gathered[kx, 1] = ritz_ref[:, half:]
+
+    pl.semaphore_wait(barrier, planes - 1)
+
+    asks = []
+    for step in range(1, planes_x):
+        ask = pltpu.make_async_remote_copy(
+            src_ref=gathered.at[kx, ex],
+            dst_ref=gathered.at[kx, ex],
+            send_sem=ritz_send.at[step - 1],
+            recv_sem=ritz_recv.at[step - 1],
+            device_id=(grp, (kx + step) % planes_x, ky, ex),
+            device_id_type=MESH,
+        )
+        ask.start()
+        asks.append(ask)
+
+    def rotate(source):
+        rows = jnp.concatenate([gathered[source, 0], gathered[source, 1]], axis=1)
+        at = pl.multiple_of(source * depth, depth)
+        return jnp.dot(
+            rows, basis_ref[pl.ds(at, depth), :], preferred_element_type=jnp.float32
+        )
+
+    total[...] = rotate(kx)
+    hands = []
+    for step in range(1, planes_x):
+        asks[step - 1].wait_recv()
+        source = (kx - step + planes_x) % planes_x
+        hand = pltpu.make_async_remote_copy(
+            src_ref=gathered.at[source, ex],
+            dst_ref=gathered.at[source, ex],
+            send_sem=fwd_send.at[step - 1],
+            recv_sem=fwd_recv.at[step - 1],
+            device_id=(grp, kx, ky, 1 - ex),
+            device_id_type=MESH,
+        )
+        hand.start()
+        hands.append(hand)
+    for step in range(1, planes_x):
+        hands[step - 1].wait_recv()
+        source = (kx - step + planes_x) % planes_x
+        total[...] += rotate(source)
+    exc_ref[...] = total[...].astype(jnp.bfloat16)
+
+    cuts = planes // tiles
+    rows_cut = count_exc // cuts
+    for tile in range(tiles):
+        moved = jnp.dot(
+            exc_ref[:, tile * LANES : (tile + 1) * LANES],
+            permute[...],
+            preferred_element_type=jnp.float32,
+        ).astype(jnp.bfloat16)
+        for cut in range(cuts):
+            slices[cut * tiles + tile] = moved[cut * rows_cut : (cut + 1) * rows_cut]
+
+    ones = []
+    for step in range(1, planes):
+        target = (me + step) % planes
+        one = pltpu.make_async_remote_copy(
+            src_ref=slices.at[target],
+            dst_ref=first.at[me],
+            send_sem=one_send.at[step - 1],
+            recv_sem=one_recv.at[step - 1],
+            device_id=device(target),
+            device_id_type=MESH,
+        )
+        one.start()
+        ones.append(one)
+    first[me] = slices[me]
+
+    own_rows = count_exc // planes_z
+    chunk = 16
+    per_block = own_rows // chunk
+
+    def mix_rows(index, carry):
+        at = pl.multiple_of(index * chunk, chunk)
+        straight = []
+        crossed = []
+        for tile in range(tiles):
+            part = exc_ref[pl.ds(at, chunk), tile * LANES : (tile + 1) * LANES].astype(jnp.float32)
+            straight.append(part)
+            crossed.append(pltpu.roll(part, LANES // 2, 1))
+        block = index // per_block
+        row = pl.multiple_of((index % per_block) * chunk, chunk)
+
+        def mix_mode(u, inner):
+            for v in range(NV):
+                for ch in range(halves):
+                    value = None
+                    for dh in range(halves):
+                        for off in range(2):
+                            factor = coefs[NV * NV + (ch * halves + dh) * 2 + off, pl.ds(u, 1), :]
+                            term = factor * (crossed if off else straight)[v * halves + dh]
+                            value = term if value is None else value + term
+                    minus = None
+                    for w in range(NV):
+                        term = coefs[w * NV + v, pl.ds(u, 1), :] * straight[w * halves + ch]
+                        minus = term if minus is None else minus + term
+                    tile = v * halves + ch
+                    mixed[block, u, pl.ds(row, chunk), tile * LANES : (tile + 1) * LANES] = (
+                        value - minus
+                    ).astype(jnp.bfloat16)
+            return inner
+
+        return lax.fori_loop(0, modes, mix_mode, carry)
+
+    lax.fori_loop(0, count_exc // chunk, mix_rows, 0)
+
+    for one in ones:
+        one.wait_recv()
+
+    def pick(target):
+        plane = wanted[pl.ds(target, 1), :]
+        value = first[0]
+        for other in range(1, planes):
+            value = jnp.where(plane == other, first[other], value)
+        return value
+
+    twos = []
+    for step in range(1, planes):
+        target = (me + step) % planes
+        second_out[target] = pick(target)
+        two = pltpu.make_async_remote_copy(
+            src_ref=second_out.at[target],
+            dst_ref=second_in.at[me],
+            send_sem=two_send.at[step - 1],
+            recv_sem=two_recv.at[step - 1],
+            device_id=device(target),
+            device_id_type=MESH,
+        )
+        two.start()
+        twos.append(two)
+    second_in[me] = pick(me)
+    for two in twos:
+        two.wait_recv()
+    for cut in range(cuts):
+        for tile in range(tiles):
+            shifted[cut * rows_cut : (cut + 1) * rows_cut, tile * LANES : (tile + 1) * LANES] = (
+                second_in[cut * tiles + tile]
+            )
+
+    def product(block):
+        left = mixed[block].reshape(modes * own_rows, tiles * LANES)
+        return lax.dot_general(
+            left, shifted[...], (((1,), (1,)), ((), ())), preferred_element_type=jnp.float32
+        )
+
+    sums = []
+    for step in range(1, planes_z):
+        block = (kz + step) % planes_z
+        sum_out[step - 1] = product(block).astype(jnp.bfloat16)
+        one_sum = pltpu.make_async_remote_copy(
+            src_ref=sum_out.at[step - 1],
+            dst_ref=sum_in.at[step - 1],
+            send_sem=a_send.at[step - 1],
+            recv_sem=a_recv.at[step - 1],
+            device_id=(grp, kx, block // 2, block % 2),
+            device_id_type=MESH,
+        )
+        one_sum.start()
+        sums.append(one_sum)
+    mine = product(kz)
+    for step in range(1, planes_z):
+        sums[step - 1].wait_recv()
+        mine = mine + sum_in[step - 1].astype(jnp.float32)
+    flipped = mine.T
+    out_rows = count_exc // planes_x
+    for block in range(planes_x):
+        turned[block] = flipped[block * out_rows : (block + 1) * out_rows]
+    lasts = []
+    for step in range(1, planes_x):
+        block = (kx + step) % planes_x
+        last_out[step - 1] = turned[block].astype(jnp.bfloat16)
+        one_last = pltpu.make_async_remote_copy(
+            src_ref=last_out.at[step - 1],
+            dst_ref=last_in.at[step - 1],
+            send_sem=b_send.at[step - 1],
+            recv_sem=b_recv.at[step - 1],
+            device_id=(grp, block, ky, ex),
+            device_id_type=MESH,
+        )
+        one_last.start()
+        lasts.append(one_last)
+    result = turned[kx]
+    for step in range(1, planes_x):
+        lasts[step - 1].wait_recv()
+        result = result + last_in[step - 1].astype(jnp.float32)
+    result = result * norm_factor
+    for u in range(modes):
+        out_ref[u] = result[:, u * own_rows : (u + 1) * own_rows]
+    for started in asks + hands + ones + twos + sums + lasts:
+        started.wait_send()
+
+
+def by_kernel(basis, ritz, phonon_g, band_index, qshift):
+    planes_x = lax.axis_size("kx")
+    planes_z = lax.axis_size(("ky", "ex"))
+    planes = planes_x * planes_z
+    count_basis, count_trans = basis.shape[0], basis.shape[3]
+    depth, count_exc = ritz.shape
+    modes = phonon_g.shape[0]
+    tiles = count_trans // LANES
+    rows_cut = count_exc // (planes // tiles)
+    own = count_exc // planes_z
+    out_rows = count_exc // planes_x
+    norm_factor = 1.0 / math.sqrt(count_trans * planes)
+    bf16 = jnp.bfloat16
+    dma = pltpu.SemaphoreType.DMA
+    vmem = pl.BlockSpec(memory_space=pltpu.VMEM)
+    smem = pl.BlockSpec(memory_space=pltpu.SMEM)
+    coefs, permute, wanted = pl.pallas_call(
+        functools.partial(tables, planes_x, planes_z),
+        out_shape=(
+            jax.ShapeDtypeStruct((NV * NV + NC * NC // 2, 8, LANES), jnp.float32),
+            jax.ShapeDtypeStruct((LANES, LANES), bf16),
+            jax.ShapeDtypeStruct((planes, LANES), jnp.int32),
+        ),
+        in_specs=[smem, smem, vmem],
+        out_specs=(vmem, vmem, vmem),
+    )(band_index, qshift, phonon_g.reshape(modes, -1))
+    return pl.pallas_call(
+        functools.partial(whole_step, planes_x, planes_z, norm_factor),
+        out_shape=jax.ShapeDtypeStruct((modes, out_rows, own), jnp.float32),
+        in_specs=[vmem] * 5,
+        out_specs=vmem,
+        scratch_shapes=[
+            pltpu.VMEM((planes_x, 2, count_exc, depth // 2), bf16),
+            pltpu.VMEM((count_exc, count_trans), jnp.float32),
+            pltpu.VMEM((count_exc, count_trans), bf16),
+            pltpu.VMEM((planes, rows_cut, LANES), bf16),
+            pltpu.VMEM((planes, rows_cut, LANES), bf16),
+            pltpu.VMEM((planes, rows_cut, LANES), bf16),
+            pltpu.VMEM((planes, rows_cut, LANES), bf16),
+            pltpu.VMEM((planes_z, modes, own, count_trans), bf16),
+            pltpu.VMEM((count_exc, count_trans), bf16),
+            pltpu.VMEM((planes_z - 1, modes * own, count_exc), bf16),
+            pltpu.VMEM((planes_z - 1, modes * own, count_exc), bf16),
+            pltpu.VMEM((planes_x, out_rows, modes * own), jnp.float32),
+            pltpu.VMEM((planes_x - 1, out_rows, modes * own), bf16),
+            pltpu.VMEM((planes_x - 1, out_rows, modes * own), bf16),
+            dma((planes_x - 1,)),
+            dma((planes_x - 1,)),
+            dma((planes_x - 1,)),
+            dma((planes_x - 1,)),
+            dma((planes - 1,)),
+            dma((planes - 1,)),
+            dma((planes - 1,)),
+            dma((planes - 1,)),
+            dma((planes_z - 1,)),
+            dma((planes_z - 1,)),
+            dma((planes_x - 1,)),
+            dma((planes_x - 1,)),
+        ],
+        compiler_params=pltpu.CompilerParams(
+            collective_id=0, has_side_effects=True, vmem_limit_bytes=40 << 20
+        ),
+    )(
+        coefs,
+        permute,
+        wanted,
+        ritz.T,
+        basis.reshape(count_basis, count_trans),
+    )
+
+
+def shards(basis, ritz, phonon_g, band_index, qshift):
+    planes_x = lax.axis_size("kx")
+    planes_z = lax.axis_size(("ky", "ex"))
+    planes = planes_x * planes_z
+    count_exc = ritz.shape[1]
+    tiles = basis.shape[3] // LANES
+    whole_tiles = (
+        basis.shape[3] == NV * NC * LANES // 2
+        and lax.axis_size("ex") == 2
+        and planes % tiles == 0
+        and count_exc % (planes // tiles * 16) == 0
+        and count_exc % (planes_z * 16) == 0
+        and count_exc % (planes_x * 16) == 0
+        and ritz.shape[0] % (2 * LANES) == 0
+        and phonon_g.shape[0] <= 8
+    )
+    step = by_kernel if whole_tiles else by_collectives
+    return step(basis, ritz, phonon_g, band_index, qshift)
+
+
 def solution(mesh):
     placed = (
         P(None, "kx", ("ky", "ex"), None),

time: 153 us -> 53.9 us (0.35); the launches traced: 150 us -> 53.5 us
  waiting for transfers between devices: 69.6 us -> 0 us
  Pallas kernels: 0 us -> 48 us
  between operations: 19.7 us -> 0.01 us
  other arithmetic: 15 us -> 0 us
  blocking collectives: 14.2 us -> 0 us
  local copies, waits for them, and re-layouts: 18.4 us -> 5.49 us
  matrix products: 9.65 us -> 0 us
  starting transfers between devices: 3.88 us -> 0 us
    pallas_call x0 -> x2, Pallas kernels: none -> 48 us  [the longest x1 46.2 us: by_kernel(): pl.pallas_call(functools.partial(whole_step, planes_x, planes_z, norm_fac...]
    ppermute x4 -> x0, waiting for transfers between devices: 25.8 us -> none  [passed_along(): return lax.ppermute(value, axis, pairs)]
    reduce_scatter x1 -> x0, waiting for transfers between devices: 25.3 us -> none  [shards(): lax.psum_scatter(partial_value, ('ky', 'ex'), scatter_dimension=2, tiled=...]
    unnamed x3 -> x0, waiting for transfers between devices: 18.4 us -> none
    all_gather x1 -> x0, blocking collectives: 14.2 us -> none  [shards(): lax.all_gather(ritz, 'kx', axis=0, tiled=True)]
    reduce_sum x1 -> x0, other arithmetic: 11.4 us -> none  [band_mix(): jnp.sum(val_mode[None, :, :, None] * amplitude[:, :, None], axis=1)]
    dot_general x11 -> x0, matrix products: 9.65 us -> none  [the longest x6 7.68 us: shards(): lax.dot_general(shifted_rows, mixed_band.reshape(count_exc, -1), (((1,),...]
    unnamed x27 -> x11, local copies, waits for them, and re-layouts: 9.81 us -> 5.49 us
  transfers between devices with their start and end apart: 6 -> 0, of which waited for: 4 -> 0; matrix products, arithmetic and copies ran while one was open for 11% -> 0% of each run, Pallas kernels for 0% -> 0%
where the time goes in v1:
time: 53.9 us; the launch traced here: 53.5 us
  Pallas kernels  48 us (89%)
  local copies, waits for them, and re-layouts  5.49 us (10%)
    pallas_call x1, Pallas kernels, by_kernel(): pl.pallas_call(functools.partial(whole_step, planes_x, planes_z, norm_fac...  46.2 us
    unnamed x11, local copies, waits for them, and re-layouts  5.49 us
    pallas_call x1, Pallas kernels, by_kernel(): pl.pallas_call(functools.partial(tables, planes_x, planes_z), out_shape=(...  1.87 us

profile of v1, /device:TPU:1, one launch (start us, length us, event | category | flops | bytes accessed | tf_op | source)
XLA Modules:
  0.0 53.5 jit_solution(7767628830111048025)
XLA Ops:
  0.0 1.9 %shard_map.55 = (f32[24,8,128]{2,1,0:T(8,128)}, bf16[128,128]{1,0:T(8,128)(2,1)}, s32[16,128]{1,0:T(8,128)}) custom-call(s32[8]{0:T(128)} %band_ref.1, s32[3]{0:T(128)} %q_ref.1, bf16[6,16384]{1,0:T(8,128)(2,1)} %bitcast.5), custom_call_target="tpu_custom_call" | custom-call | tf_op jit(solution)/shard_map/pallas_call | solution.py:380
  1.9 0.0 copy-start
  1.9 1.6 %copy-done = bf16[1024,1,1,1024]{3,0,2,1:T(8,128)(2,1)S(1)} copy-done((bf16[1024,1,1,1024]{3,0,2,1:T(8,128)(2,1)S(1)}, bf16[1024,1,1,1024]{3,0,2,1:T(8,128)(2,1)}, u32[]{:S(2)}) %copy-start) | copy-done | bytes 2097176
  3.5 0.0 copy-start.1
  3.5 0.9 %copy-done.1 = bf16[256,192]{0,1:T(8,128)(2,1)S(1)} copy-done((bf16[256,192]{0,1:T(8,128)(2,1)S(1)}, bf16[256,192]{0,1:T(8,128)(2,1)}, u32[]{:S(2)}) %copy-start.1) | copy-done | bytes 98328
  4.4 0.0 copy-start.2
  4.4 0.9 %copy-done.2 = f32[24,8,128]{2,1,0:T(8,128)S(1)} copy-done((f32[24,8,128]{2,1,0:T(8,128)S(1)}, f32[24,8,128]{2,1,0:T(8,128)}, u32[]{:S(2)}) %copy-start.2) | copy-done | bytes 98328
  5.3 0.0 copy-start.3
  5.3 0.8 %copy-done.3 = bf16[128,128]{1,0:T(8,128)(2,1)S(1)} copy-done((bf16[128,128]{1,0:T(8,128)(2,1)S(1)}, bf16[128,128]{1,0:T(8,128)(2,1)}, u32[]{:S(2)}) %copy-start.3) | copy-done | bytes 32792
  6.0 0.0 copy-start.4
  6.0 0.7 %copy-done.4 = s32[16,128]{1,0:T(8,128)S(1)} copy-done((s32[16,128]{1,0:T(8,128)S(1)}, s32[16,128]{1,0:T(8,128)}, u32[]{:S(2)}) %copy-start.4) | copy-done | bytes 8216
  6.7 46.2 %shard_map.56 = f32[6,48,48]{2,1,0:T(8,128)S(1)} custom-call(f32[24,8,128]{2,1,0:T(8,128)S(1)} %copy-done.2, bf16[128,128]{1,0:T(8,128)(2,1)S(1)} %copy-done.3, s32[16,128]{1,0:T(8,128)S(1)} %copy-done.4, bf16[192,256]{1,0:T(8,128)(2,1)S(1)} %bitcast.4, bf16[1024,1024]{1,0:T(8,128)(2,1)S(1)} %bitcast.3), custom_call_target="tpu_custom_call" | custom-call | tf_op jit(solution)/shard_map/pallas_call | solution.py:390
  52.9 0.7 %copy.7 = f32[6,48,48]{2,1,0:T(8,128)} copy(f32[6,48,48]{2,1,0:T(8,128)S(1)} %shard_map.56) | data formatting | bytes 110592
Async XLA Ops:
  1.9 1.6 %copy-start = (bf16[1024,1,1,1024]{3,0,2,1:T(8,128)(2,1)S(1)}, bf16[1024,1,1,1024]{3,0,2,1:T(8,128)(2,1)}, u32[]{:S(2)}) copy-start(bf16[1024,1,1,1024]{3,0,2,1:T(8,128)(2,1)} %param.5) | copy-start | bytes 6291460
  3.5 0.9 %copy-start.1 = (bf16[256,192]{0,1:T(8,128)(2,1)S(1)}, bf16[256,192]{0,1:T(8,128)(2,1)}, u32[]{:S(2)}) copy-start(bf16[256,192]{0,1:T(8,128)(2,1)} %param.6) | copy-start | bytes 294916
  4.4 0.9 %copy-start.2 = (f32[24,8,128]{2,1,0:T(8,128)S(1)}, f32[24,8,128]{2,1,0:T(8,128)}, u32[]{:S(2)}) copy-start(f32[24,8,128]{2,1,0:T(8,128)} %get-tuple-element.8.coefs) | copy-start | bytes 294916
  5.3 0.8 %copy-start.3 = (bf16[128,128]{1,0:T(8,128)(2,1)S(1)}, bf16[128,128]{1,0:T(8,128)(2,1)}, u32[]{:S(2)}) copy-start(bf16[128,128]{1,0:T(8,128)(2,1)} %get-tuple-element.9.permute) | copy-start | bytes 98308
  6.0 0.7 %copy-start.4 = (s32[16,128]{1,0:T(8,128)S(1)}, s32[16,128]{1,0:T(8,128)}, u32[]{:S(2)}) copy-start(s32[16,128]{1,0:T(8,128)} %get-tuple-element.10.wanted) | copy-start | bytes 24580

commit v2 on v1

--- a/solution.py
+++ b/solution.py
@@ -98,49 +98,12 @@
     return coupling * norm_factor
 
 
-def tables(planes_x, planes_z, band_ref, q_ref, phonon_ref, coefs, permute, wanted):
-    modes = phonon_ref.shape[0]
-    halves = NC // 2
-    lane = lax.broadcasted_iota(jnp.int32, (modes, LANES), 1)
-    low = lane < LANES // 2
-
-    def on_both(left, right):
-        row = band_ref[left] * ALLB + band_ref[right]
-        at = pl.multiple_of((row // 2) * LANES, LANES)
-        tile = phonon_ref[:, pl.ds(at, LANES)].astype(jnp.float32)
-        other = pltpu.roll(tile, LANES // 2, 1)
-        odd = row % 2
-        return jnp.where(low == (odd == 0), tile, other)
-
-    for w in range(NV):
-        for v in range(NV):
-            coefs[w * NV + v, :modes, :] = on_both(w, v)
-    for ch in range(halves):
-        for dh in range(halves):
-            for off in range(2):
-                lower = on_both(NV + 2 * ch, NV + 2 * dh + off)
-                upper = on_both(NV + 2 * ch + 1, NV + 2 * dh + 1 - off)
-                place = NV * NV + (ch * halves + dh) * 2 + off
-                coefs[place, :modes, :] = jnp.where(low, lower, upper)
-
-    come = lax.broadcasted_iota(jnp.int32, (LANES, LANES), 0)
-    goes = lax.broadcasted_iota(jnp.int32, (LANES, LANES), 1)
-    width = LANES // 2
-    source = (goes // width) * width + (goes % width + q_ref[1]) % width
-    permute[...] = (come == source).astype(jnp.bfloat16)
-
-    for target in range(planes_x * planes_z):
-        x = (target // planes_z + q_ref[0]) % planes_x
-        z = (target % planes_z + q_ref[2]) % planes_z
-        wanted[target : target + 1, :] = jnp.full((1, LANES), x * planes_z + z, jnp.int32)
-
-
 def whole_step(
     planes_x, planes_z, norm_factor,
-    coefs, permute, wanted, ritz_ref, basis_ref, out_ref,
-    gathered, total, exc_ref, slices, first, second_out, second_in,
+    band_hbm, q_hbm, ritz_hbm, phonon_hbm, basis_hbm, out_ref,
+    band_ref, q_ref, ritz_ref, phonon_ref, basis_ref, coefs, gathered, total, exc_ref, slices, first, second_out, second_in,
     mixed, shifted, sum_out, sum_in, turned, last_out, last_in,
-    ritz_send, ritz_recv, fwd_send, fwd_recv,
+    load_sems, ritz_send, ritz_recv, fwd_send, fwd_recv,
     one_send, one_recv, two_send, two_recv, a_send, a_recv, b_send, b_recv,
 ):
     planes = planes_x * planes_z
@@ -165,9 +128,23 @@
         pl.semaphore_signal(
             barrier, inc=1, device_id=device((me + step) % planes), device_id_type=MESH
         )
+    loads = [
+        pltpu.make_async_copy(source, place, load_sems.at[at])
+        for at, (source, place) in enumerate(
+            (
+                (ritz_hbm, ritz_ref),
+                (band_hbm, band_ref),
+                (q_hbm, q_ref),
+                (phonon_hbm, phonon_ref),
+                (basis_hbm, basis_ref),
+            )
+        )
+    ]
+    for load in loads:
+        load.start()
+    loads[0].wait()
     gathered[kx, 0] = ritz_ref[:, :half]
     gathered[kx, 1] = ritz_ref[:, half:]
-
     pl.semaphore_wait(barrier, planes - 1)
 
     asks = []
@@ -182,6 +159,53 @@
         )
         ask.start()
         asks.append(ask)
+
+    for load in loads[1:4]:
+        load.wait()
+    lane = lax.broadcasted_iota(jnp.int32, (modes, LANES), 1)
+    low = lane < LANES // 2
+    bands = [jnp.full((modes, LANES), band_ref[slot], jnp.int32) for slot in range(NV + NC)]
+    part = ALLB // 2
+    row_tiles = part // 2
+
+    def rows_of(slot, base):
+        found = []
+        for at in range(row_tiles):
+            value = None
+            for band in range(base, base + part):
+                start = (band * part + base // 2 + at) * LANES
+                tile = phonon_ref[:, start : start + LANES].astype(jnp.float32)
+                value = tile if value is None else jnp.where(bands[slot] == band, tile, value)
+            found.append(value)
+        return found
+
+    def on_both(found, slot, base):
+        value = found[0]
+        for at in range(1, row_tiles):
+            value = jnp.where((bands[slot] >> 1) == base // 2 + at, found[at], value)
+        other = pltpu.roll(value, LANES // 2, 1)
+        upper = (bands[slot] & 1) == jnp.where(low, 0, 1)
+        return jnp.where(upper, value, other)
+
+    for w in range(NV):
+        found = rows_of(w, 0)
+        for v in range(NV):
+            coefs[w * NV + v, :modes, :] = on_both(found, v, 0)
+    for ch in range(halves):
+        lower_rows = rows_of(NV + 2 * ch, part)
+        upper_rows = rows_of(NV + 2 * ch + 1, part)
+        for dh in range(halves):
+            for off in range(2):
+                lower = on_both(lower_rows, NV + 2 * dh + off, part)
+                upper = on_both(upper_rows, NV + 2 * dh + 1 - off, part)
+                place = NV * NV + (ch * halves + dh) * 2 + off
+                coefs[place, :modes, :] = jnp.where(low, lower, upper)
+    come = lax.broadcasted_iota(jnp.int32, (LANES, LANES), 0)
+    goes = lax.broadcasted_iota(jnp.int32, (LANES, LANES), 1)
+    width = LANES // 2
+    along = jnp.full((LANES, LANES), q_ref[1], jnp.int32)
+    permute = (come == (goes & width) + ((goes + along) & (width - 1))).astype(jnp.bfloat16)
+    loads[4].wait()
 
     def rotate(source):
         rows = jnp.concatenate([gathered[source, 0], gathered[source, 1]], axis=1)
@@ -216,7 +240,7 @@
     for tile in range(tiles):
         moved = jnp.dot(
             exc_ref[:, tile * LANES : (tile + 1) * LANES],
-            permute[...],
+            permute,
             preferred_element_type=jnp.float32,
         ).astype(jnp.bfloat16)
         for cut in range(cuts):
@@ -278,11 +302,20 @@
     for one in ones:
         one.wait_recv()
 
+    along_x = jnp.full((1, LANES), q_ref[0], jnp.int32)
+    along_z = jnp.full((1, LANES), q_ref[2], jnp.int32)
+
     def pick(target):
-        plane = wanted[pl.ds(target, 1), :]
-        value = first[0]
-        for other in range(1, planes):
-            value = jnp.where(plane == other, first[other], value)
+        x, z = target // planes_z, target % planes_z
+        value = None
+        for dx in range(1, planes_x):
+            for dz in range(1, planes_z):
+                plane = ((x + dx) % planes_x) * planes_z + (z + dz) % planes_z
+                there = first[plane]
+                if value is None:
+                    value = there
+                else:
+                    value = jnp.where((along_x == dx) & (along_z == dz), there, value)
         return value
 
     twos = []
@@ -376,23 +409,19 @@
     bf16 = jnp.bfloat16
     dma = pltpu.SemaphoreType.DMA
     vmem = pl.BlockSpec(memory_space=pltpu.VMEM)
-    smem = pl.BlockSpec(memory_space=pltpu.SMEM)
-    coefs, permute, wanted = pl.pallas_call(
-        functools.partial(tables, planes_x, planes_z),
-        out_shape=(
-            jax.ShapeDtypeStruct((NV * NV + NC * NC // 2, 8, LANES), jnp.float32),
-            jax.ShapeDtypeStruct((LANES, LANES), bf16),
-            jax.ShapeDtypeStruct((planes, LANES), jnp.int32),
-        ),
-        in_specs=[smem, smem, vmem],
-        out_specs=(vmem, vmem, vmem),
-    )(band_index, qshift, phonon_g.reshape(modes, -1))
+    stay = pl.BlockSpec(memory_space=pl.ANY)
     return pl.pallas_call(
         functools.partial(whole_step, planes_x, planes_z, norm_factor),
         out_shape=jax.ShapeDtypeStruct((modes, out_rows, own), jnp.float32),
-        in_specs=[vmem] * 5,
+        in_specs=[stay] * 5,
         out_specs=vmem,
         scratch_shapes=[
+            pltpu.SMEM(band_index.shape, jnp.int32),
+            pltpu.SMEM(qshift.shape, jnp.int32),
+            pltpu.VMEM((count_exc, depth), bf16),
+            pltpu.VMEM((modes, phonon_g.shape[3]), bf16),
+            pltpu.VMEM((count_basis, count_trans), bf16),
+            pltpu.VMEM((NV * NV + NC * NC // 2, 8, LANES), jnp.float32),
             pltpu.VMEM((planes_x, 2, count_exc, depth // 2), bf16),
             pltpu.VMEM((count_exc, count_trans), jnp.float32),
             pltpu.VMEM((count_exc, count_trans), bf16),
@@ -407,6 +436,7 @@
             pltpu.VMEM((planes_x, out_rows, modes * own), jnp.float32),
             pltpu.VMEM((planes_x - 1, out_rows, modes * own), bf16),
             pltpu.VMEM((planes_x - 1, out_rows, modes * own), bf16),
+            dma((5,)),
             dma((planes_x - 1,)),
             dma((planes_x - 1,)),
             dma((planes_x - 1,)),
@@ -421,13 +451,13 @@
             dma((planes_x - 1,)),
         ],
         compiler_params=pltpu.CompilerParams(
-            collective_id=0, has_side_effects=True, vmem_limit_bytes=40 << 20
+            collective_id=0, has_side_effects=True, vmem_limit_bytes=60 << 20
         ),
     )(
-        coefs,
-        permute,
-        wanted,
+        band_index,
+        qshift,
         ritz.T,
+        phonon_g.reshape(modes, -1),
         basis.reshape(count_basis, count_trans),
     )
 

time: 53.9 us -> 48.9 us (0.907)
  local copies, waits for them, and re-layouts: 5.49 us -> 1.58 us
  Pallas kernels: 48 us -> 47.2 us
    unnamed x11 -> x1, local copies, waits for them, and re-layouts: 5.49 us -> 1.58 us
    pallas_call x1 -> x0, Pallas kernels: 1.87 us -> none  [by_kernel(): pl.pallas_call(functools.partial(tables, planes_x, planes_z), out_shape=(...]
    pallas_call x1, Pallas kernels: 46.2 us -> 47.2 us  [by_kernel(): pl.pallas_call(functools.partial(whole_step, planes_x, planes_z, norm_fac...]
where the time goes in v2:
time: 48.9 us; the launch traced here: 48.7 us
  Pallas kernels  47.2 us (97%)
  local copies, waits for them, and re-layouts  1.58 us (3%)
    pallas_call x1, Pallas kernels, by_kernel(): pl.pallas_call(functools.partial(whole_step, planes_x, planes_z, norm_fac...  47.2 us
    unnamed x1, local copies, waits for them, and re-layouts  1.58 us

profile of v2, /device:TPU:1, one launch (start us, length us, event | category | flops | bytes accessed | tf_op | source)
XLA Modules:
  0.0 48.7 jit_solution(4895543348712932973)
XLA Ops:
  0.0 47.2 %shard_map.55 = f32[6,48,48]{2,1,0:T(8,128)} custom-call(s32[8]{0:T(128)} %band_hbm.1, s32[3]{0:T(128)} %q_hbm.1, bf16[192,256]{1,0:T(8,128)(2,1)} %bitcast.5, bf16[6,16384]{1,0:T(8,128)(2,1)} %bitcast.4, bf16[1024,1024]{1,0:T(8,128)(2,1)} %bitcast.3), custom_call_target="tpu_custom_call" | custom-call | tf_op jit(solution)/shard_map/pallas_call | solution.py:413
  47.2 1.6 %copy.7 = f32[6,48,48]{2,1,0:T(8,128)} copy(f32[6,48,48]{2,1,0:T(8,128)} %shard_map.55) | data formatting | bytes 110592

commit v3 on v2

--- a/solution.py
+++ b/solution.py
@@ -237,6 +237,7 @@
 
     cuts = planes // tiles
     rows_cut = count_exc // cuts
+    rows_half = rows_cut // 2
     for tile in range(tiles):
         moved = jnp.dot(
             exc_ref[:, tile * LANES : (tile + 1) * LANES],
@@ -244,7 +245,9 @@
             preferred_element_type=jnp.float32,
         ).astype(jnp.bfloat16)
         for cut in range(cuts):
-            slices[cut * tiles + tile] = moved[cut * rows_cut : (cut + 1) * rows_cut]
+            for part_of in range(2):
+                at = cut * rows_cut + part_of * rows_half
+                slices[cut * tiles + tile, part_of] = moved[at : at + rows_half]
 
     ones = []
     for step in range(1, planes):
@@ -305,13 +308,13 @@
     along_x = jnp.full((1, LANES), q_ref[0], jnp.int32)
     along_z = jnp.full((1, LANES), q_ref[2], jnp.int32)
 
-    def pick(target):
+    def pick(target, part_of):
         x, z = target // planes_z, target % planes_z
         value = None
         for dx in range(1, planes_x):
             for dz in range(1, planes_z):
                 plane = ((x + dx) % planes_x) * planes_z + (z + dz) % planes_z
-                there = first[plane]
+                there = first[plane, part_of]
                 if value is None:
                     value = there
                 else:
@@ -319,78 +322,84 @@
         return value
 
     twos = []
-    for step in range(1, planes):
-        target = (me + step) % planes
-        second_out[target] = pick(target)
-        two = pltpu.make_async_remote_copy(
-            src_ref=second_out.at[target],
-            dst_ref=second_in.at[me],
-            send_sem=two_send.at[step - 1],
-            recv_sem=two_recv.at[step - 1],
-            device_id=device(target),
-            device_id_type=MESH,
-        )
-        two.start()
-        twos.append(two)
-    second_in[me] = pick(me)
-    for two in twos:
-        two.wait_recv()
-    for cut in range(cuts):
-        for tile in range(tiles):
-            shifted[cut * rows_cut : (cut + 1) * rows_cut, tile * LANES : (tile + 1) * LANES] = (
-                second_in[cut * tiles + tile]
+    for order in range(2):
+        for step in range(1, planes):
+            target = (me + step) % planes
+            part_of = (target // planes_z + order + 1) % 2
+            second_out[target, order] = pick(target, part_of)
+            at = order * (planes - 1) + step - 1
+            two = pltpu.make_async_remote_copy(
+                src_ref=second_out.at[target, order],
+                dst_ref=second_in.at[me, order],
+                send_sem=two_send.at[at],
+                recv_sem=two_recv.at[at],
+                device_id=device(target),
+                device_id_type=MESH,
             )
-
-    def product(block):
-        left = mixed[block].reshape(modes * own_rows, tiles * LANES)
+            two.start()
+            twos.append(two)
+        second_in[me, order] = pick(me, (kx + order + 1) % 2)
+
+    def product(order, block):
+        right = mixed[block].reshape(modes * own_rows, tiles * LANES)
         return lax.dot_general(
-            left, shifted[...], (((1,), (1,)), ((), ())), preferred_element_type=jnp.float32
+            shifted[order], right, (((1,), (1,)), ((), ())), preferred_element_type=jnp.float32
         )
 
     sums = []
-    for step in range(1, planes_z):
-        block = (kz + step) % planes_z
-        sum_out[step - 1] = product(block).astype(jnp.bfloat16)
-        one_sum = pltpu.make_async_remote_copy(
-            src_ref=sum_out.at[step - 1],
-            dst_ref=sum_in.at[step - 1],
-            send_sem=a_send.at[step - 1],
-            recv_sem=a_recv.at[step - 1],
-            device_id=(grp, kx, block // 2, block % 2),
-            device_id_type=MESH,
-        )
-        one_sum.start()
-        sums.append(one_sum)
-    mine = product(kz)
-    for step in range(1, planes_z):
-        sums[step - 1].wait_recv()
-        mine = mine + sum_in[step - 1].astype(jnp.float32)
-    flipped = mine.T
-    out_rows = count_exc // planes_x
-    for block in range(planes_x):
-        turned[block] = flipped[block * out_rows : (block + 1) * out_rows]
+    mine = []
+    for order in range(2):
+        for two in twos[order * (planes - 1) : (order + 1) * (planes - 1)]:
+            two.wait_recv()
+        for cut in range(cuts):
+            for tile in range(tiles):
+                rows = slice(cut * rows_half, (cut + 1) * rows_half)
+                lanes = slice(tile * LANES, (tile + 1) * LANES)
+                shifted[order, rows, lanes] = second_in[cut * tiles + tile, order]
+        for step in range(1, planes_z):
+            block = (kz + step) % planes_z
+            at = order * (planes_z - 1) + step - 1
+            sum_out[at] = product(order, block).astype(jnp.bfloat16)
+            one_sum = pltpu.make_async_remote_copy(
+                src_ref=sum_out.at[at],
+                dst_ref=sum_in.at[at],
+                send_sem=a_send.at[at],
+                recv_sem=a_recv.at[at],
+                device_id=(grp, kx, block // 2, block % 2),
+                device_id_type=MESH,
+            )
+            one_sum.start()
+            sums.append(one_sum)
+        mine.append(product(order, kz))
     lasts = []
-    for step in range(1, planes_x):
-        block = (kx + step) % planes_x
-        last_out[step - 1] = turned[block].astype(jnp.bfloat16)
-        one_last = pltpu.make_async_remote_copy(
-            src_ref=last_out.at[step - 1],
-            dst_ref=last_in.at[step - 1],
-            send_sem=b_send.at[step - 1],
-            recv_sem=b_recv.at[step - 1],
-            device_id=(grp, block, ky, ex),
-            device_id_type=MESH,
-        )
-        one_last.start()
-        lasts.append(one_last)
-    result = turned[kx]
-    for step in range(1, planes_x):
-        lasts[step - 1].wait_recv()
+    for order in range(2):
+        value = mine[order]
+        for at in range(order * (planes_z - 1), (order + 1) * (planes_z - 1)):
+            sums[at].wait_recv()
+            value = value + sum_in[at].astype(jnp.float32)
+        for cut in range(cuts):
+            turned[order, cut] = value[cut * rows_half : (cut + 1) * rows_half]
+        for step in range(1 + order, planes_x, 2):
+            block = (kx + step) % planes_x
+            last_out[step - 1] = turned[order, block // 2].astype(jnp.bfloat16)
+            one_last = pltpu.make_async_remote_copy(
+                src_ref=last_out.at[step - 1],
+                dst_ref=last_in.at[step - 1],
+                send_sem=b_send.at[step - 1],
+                recv_sem=b_recv.at[step - 1],
+                device_id=(grp, block, ky, ex),
+                device_id_type=MESH,
+            )
+            one_last.start()
+            lasts.append((step, one_last))
+    result = turned[1, kx // 2]
+    for step, one_last in lasts:
+        one_last.wait_recv()
         result = result + last_in[step - 1].astype(jnp.float32)
     result = result * norm_factor
     for u in range(modes):
         out_ref[u] = result[:, u * own_rows : (u + 1) * own_rows]
-    for started in asks + hands + ones + twos + sums + lasts:
+    for started in asks + hands + ones + twos + sums + [last for step, last in lasts]:
         started.wait_send()
 
 
@@ -425,15 +434,15 @@
             pltpu.VMEM((planes_x, 2, count_exc, depth // 2), bf16),
             pltpu.VMEM((count_exc, count_trans), jnp.float32),
             pltpu.VMEM((count_exc, count_trans), bf16),
-            pltpu.VMEM((planes, rows_cut, LANES), bf16),
-            pltpu.VMEM((planes, rows_cut, LANES), bf16),
-            pltpu.VMEM((planes, rows_cut, LANES), bf16),
-            pltpu.VMEM((planes, rows_cut, LANES), bf16),
+            pltpu.VMEM((planes, 2, rows_cut // 2, LANES), bf16),
+            pltpu.VMEM((planes, 2, rows_cut // 2, LANES), bf16),
+            pltpu.VMEM((planes, 2, rows_cut // 2, LANES), bf16),
+            pltpu.VMEM((planes, 2, rows_cut // 2, LANES), bf16),
             pltpu.VMEM((planes_z, modes, own, count_trans), bf16),
-            pltpu.VMEM((count_exc, count_trans), bf16),
-            pltpu.VMEM((planes_z - 1, modes * own, count_exc), bf16),
-            pltpu.VMEM((planes_z - 1, modes * own, count_exc), bf16),
-            pltpu.VMEM((planes_x, out_rows, modes * own), jnp.float32),
+            pltpu.VMEM((2, count_exc // 2, count_trans), bf16),
+            pltpu.VMEM((2 * (planes_z - 1), count_exc // 2, modes * own), bf16),
+            pltpu.VMEM((2 * (planes_z - 1), count_exc // 2, modes * own), bf16),
+            pltpu.VMEM((2, planes_x // 2, out_rows, modes * own), jnp.float32),
             pltpu.VMEM((planes_x - 1, out_rows, modes * own), bf16),
             pltpu.VMEM((planes_x - 1, out_rows, modes * own), bf16),
             dma((5,)),
@@ -443,10 +452,10 @@
             dma((planes_x - 1,)),
             dma((planes - 1,)),
             dma((planes - 1,)),
-            dma((planes - 1,)),
-            dma((planes - 1,)),
-            dma((planes_z - 1,)),
-            dma((planes_z - 1,)),
+            dma((2 * (planes - 1),)),
+            dma((2 * (planes - 1),)),
+            dma((2 * (planes_z - 1),)),
+            dma((2 * (planes_z - 1),)),
             dma((planes_x - 1,)),
             dma((planes_x - 1,)),
         ],
@@ -472,7 +481,8 @@
         basis.shape[3] == NV * NC * LANES // 2
         and lax.axis_size("ex") == 2
         and planes % tiles == 0
-        and count_exc % (planes // tiles * 16) == 0
+        and planes_x * tiles == 2 * planes
+        and count_exc % (planes // tiles * 32) == 0
         and count_exc % (planes_z * 16) == 0
         and count_exc % (planes_x * 16) == 0
         and ritz.shape[0] % (2 * LANES) == 0

time: 48.9 us -> 46.6 us (0.953)
  Pallas kernels: 47.2 us -> 44.6 us
    pallas_call x1, Pallas kernels: 47.2 us -> 44.6 us  [by_kernel(): pl.pallas_call(functools.partial(whole_step, planes_x, planes_z, norm_fac...]
where the time goes in v3:
time: 46.6 us; the launch traced here: 46.2 us
  Pallas kernels  44.6 us (96%)
  local copies, waits for them, and re-layouts  1.58 us (3%)
    pallas_call x1, Pallas kernels, by_kernel(): pl.pallas_call(functools.partial(whole_step, planes_x, planes_z, norm_fac...  44.6 us
    unnamed x1, local copies, waits for them, and re-layouts  1.58 us

profile of v3, /device:TPU:1, one launch (start us, length us, event | category | flops | bytes accessed | tf_op | source)
XLA Modules:
  0.0 46.2 jit_solution(1673970484861863089)
XLA Ops:
  0.0 44.6 %shard_map.55 = f32[6,48,48]{2,1,0:T(8,128)} custom-call(s32[8]{0:T(128)} %band_hbm.1, s32[3]{0:T(128)} %q_hbm.1, bf16[192,256]{1,0:T(8,128)(2,1)} %bitcast.5, bf16[6,16384]{1,0:T(8,128)(2,1)} %bitcast.4, bf16[1024,1024]{1,0:T(8,128)(2,1)} %bitcast.3), custom_call_target="tpu_custom_call" | custom-call | tf_op jit(solution)/shard_map/pallas_call | solution.py:422
  44.6 1.6 %copy.7 = f32[6,48,48]{2,1,0:T(8,128)} copy(f32[6,48,48]{2,1,0:T(8,128)} %shard_map.55) | data formatting | bytes 110592

commit v4 on v3

--- a/solution.py
+++ b/solution.py
@@ -101,9 +101,9 @@
 def whole_step(
     planes_x, planes_z, norm_factor,
     band_hbm, q_hbm, ritz_hbm, phonon_hbm, basis_hbm, out_ref,
-    band_ref, q_ref, ritz_ref, phonon_ref, basis_ref, coefs, gathered, total, exc_ref, slices, first, second_out, second_in,
+    band_ref, q_ref, ritz_ref, phonon_ref, basis_ref, coefs, gathered, total, exc_ref, slices, first, second_out, second_in, shifts,
     mixed, shifted, sum_out, sum_in, turned, last_out, last_in,
-    load_sems, ritz_send, ritz_recv, fwd_send, fwd_recv,
+    load_sems, swap_sems, ritz_send, ritz_recv, fwd_send, fwd_recv,
     one_send, one_recv, two_send, two_recv, a_send, a_recv, b_send, b_recv,
 ):
     planes = planes_x * planes_z
@@ -119,14 +119,17 @@
     tiles = exc_ref.shape[1] // LANES
     halves = NC // 2
 
-    def device(plane):
+    def device(plane, group):
         z = plane % planes_z
-        return (grp, plane // planes_z, z // 2, z % 2)
+        return (group, plane // planes_z, z // 2, z % 2)
 
     barrier = pltpu.get_barrier_semaphore()
-    for step in range(1, planes):
+    for step in range(1, 2 * planes):
         pl.semaphore_signal(
-            barrier, inc=1, device_id=device((me + step) % planes), device_id_type=MESH
+            barrier,
+            inc=1,
+            device_id=device((me + step) % planes, (grp + step // planes) % 2),
+            device_id_type=MESH,
         )
     loads = [
         pltpu.make_async_copy(source, place, load_sems.at[at])
@@ -145,7 +148,7 @@
     loads[0].wait()
     gathered[kx, 0] = ritz_ref[:, :half]
     gathered[kx, 1] = ritz_ref[:, half:]
-    pl.semaphore_wait(barrier, planes - 1)
+    pl.semaphore_wait(barrier, 2 * planes - 1)
 
     asks = []
     for step in range(1, planes_x):
@@ -162,6 +165,19 @@
 
     for load in loads[1:4]:
         load.wait()
+    first_row = lax.broadcasted_iota(jnp.int32, (8, LANES), 0) == 0
+    along_x = jnp.full((8, LANES), q_ref[0], jnp.int32)
+    along_z = jnp.full((8, LANES), q_ref[2], jnp.int32)
+    shifts[grp] = jnp.where(first_row, along_x, along_z)
+    swap = pltpu.make_async_remote_copy(
+        src_ref=shifts.at[grp],
+        dst_ref=shifts.at[grp],
+        send_sem=swap_sems.at[0],
+        recv_sem=swap_sems.at[1],
+        device_id=(1 - grp, kx, ky, ex),
+        device_id_type=MESH,
+    )
+    swap.start()
     lane = lax.broadcasted_iota(jnp.int32, (modes, LANES), 1)
     low = lane < LANES // 2
     bands = [jnp.full((modes, LANES), band_ref[slot], jnp.int32) for slot in range(NV + NC)]
@@ -239,11 +255,7 @@
     rows_cut = count_exc // cuts
     rows_half = rows_cut // 2
     for tile in range(tiles):
-        moved = jnp.dot(
-            exc_ref[:, tile * LANES : (tile + 1) * LANES],
-            permute,
-            preferred_element_type=jnp.float32,
-        ).astype(jnp.bfloat16)
+        moved = exc_ref[:, tile * LANES : (tile + 1) * LANES]
         for cut in range(cuts):
             for part_of in range(2):
                 at = cut * rows_cut + part_of * rows_half
@@ -253,16 +265,16 @@
     for step in range(1, planes):
         target = (me + step) % planes
         one = pltpu.make_async_remote_copy(
-            src_ref=slices.at[target],
+            src_ref=slices.at[target, grp],
             dst_ref=first.at[me],
             send_sem=one_send.at[step - 1],
             recv_sem=one_recv.at[step - 1],
-            device_id=device(target),
+            device_id=device(target, grp),
             device_id_type=MESH,
         )
         one.start()
         ones.append(one)
-    first[me] = slices[me]
+    first[me] = slices[me, grp]
 
     own_rows = count_exc // planes_z
     chunk = 16
@@ -300,45 +312,60 @@
 
         return lax.fori_loop(0, modes, mix_mode, carry)
 
-    lax.fori_loop(0, count_exc // chunk, mix_rows, 0)
+    chunks = count_exc // chunk
+    lax.fori_loop(0, chunks // 2, mix_rows, 0)
 
     for one in ones:
         one.wait_recv()
 
-    along_x = jnp.full((1, LANES), q_ref[0], jnp.int32)
-    along_z = jnp.full((1, LANES), q_ref[2], jnp.int32)
-
-    def pick(target, part_of):
-        x, z = target // planes_z, target % planes_z
+    swap.wait_recv()
+
+    def pick(x, z, group):
+        row_x = shifts[group, 0:1, :]
+        row_z = shifts[group, 1:2, :]
         value = None
         for dx in range(1, planes_x):
             for dz in range(1, planes_z):
-                plane = ((x + dx) % planes_x) * planes_z + (z + dz) % planes_z
-                there = first[plane, part_of]
+                there = first[((x + dx) % planes_x) * planes_z + (z + dz) % planes_z]
                 if value is None:
                     value = there
                 else:
-                    value = jnp.where((along_x == dx) & (along_z == dz), there, value)
+                    value = jnp.where((row_x == dx) & (row_z == dz), there, value)
         return value
 
-    twos = []
-    for order in range(2):
-        for step in range(1, planes):
-            target = (me + step) % planes
-            part_of = (target // planes_z + order + 1) % 2
-            second_out[target, order] = pick(target, part_of)
-            at = order * (planes - 1) + step - 1
-            two = pltpu.make_async_remote_copy(
-                src_ref=second_out.at[target, order],
-                dst_ref=second_in.at[me, order],
-                send_sem=two_send.at[at],
-                recv_sem=two_recv.at[at],
-                device_id=device(target),
-                device_id_type=MESH,
-            )
-            two.start()
-            twos.append(two)
-        second_in[me, order] = pick(me, (kx + order + 1) % 2)
+    def second(dx, dz, dg):
+        x, z, group = (kx + dx) % planes_x, (kz + dz) % planes_z, (grp + dg) % 2
+        plane = x * planes_z + z
+        at = (dg * planes_x + dx) * planes_z + dz
+        return pltpu.make_async_remote_copy(
+            src_ref=second_out.at[group, plane],
+            dst_ref=second_in.at[grp, me],
+            send_sem=two_send.at[at],
+            recv_sem=two_recv.at[at],
+            device_id=device(plane, group),
+            device_id_type=MESH,
+        )
+
+    def send_second(dx, dz, dg):
+        x, z, group = (kx + dx) % planes_x, (kz + dz) % planes_z, (grp + dg) % 2
+        second_out[group, x * planes_z + z] = pick(x, z, group)
+        second(dx, dz, dg).start()
+
+    def others(parity, act):
+        for far in reversed(range(planes_x // 2)):
+            dx = 2 * far + parity
+            for dz in range(planes_z):
+                for dg in (1, 0):
+                    if far == 0 and dz == 0 and dg == 0:
+                        pl.when(parity != 0)(functools.partial(act, dx, dz, dg))
+                    else:
+                        act(dx, dz, dg)
+
+    early = (grp + kx + 1) % 2
+    others(early, send_second)
+    others(1 - early, send_second)
+    second_in[grp, me] = pick(kx, kz, grp)
+    lax.fori_loop(chunks // 2, chunks, mix_rows, 0)
 
     def product(order, block):
         right = mixed[block].reshape(modes * own_rows, tiles * LANES)
@@ -349,13 +376,21 @@
     sums = []
     mine = []
     for order in range(2):
-        for two in twos[order * (planes - 1) : (order + 1) * (planes - 1)]:
-            two.wait_recv()
-        for cut in range(cuts):
-            for tile in range(tiles):
-                rows = slice(cut * rows_half, (cut + 1) * rows_half)
-                lanes = slice(tile * LANES, (tile + 1) * LANES)
-                shifted[order, rows, lanes] = second_in[cut * tiles + tile, order]
+        half_of = (kx + order + 1) % 2
+        for step in range(1, planes_x * planes_z + 1):
+            dx, dz = (step // planes_z) % planes_x, step % planes_z
+            dg = (grp + half_of) % 2
+            if dx or dz:
+                second(dx, dz, dg).wait_recv()
+            else:
+                pl.when(dg != 0)(lambda dg=dg: second(0, 0, dg).wait_recv())
+        for tile in range(tiles):
+            came = jnp.concatenate(
+                [second_in[half_of, cut * tiles + tile] for cut in range(cuts)], axis=0
+            )
+            shifted[order, :, tile * LANES : (tile + 1) * LANES] = jnp.dot(
+                came, permute, preferred_element_type=jnp.float32
+            ).astype(jnp.bfloat16)
         for step in range(1, planes_z):
             block = (kz + step) % planes_z
             at = order * (planes_z - 1) + step - 1
@@ -399,8 +434,10 @@
     result = result * norm_factor
     for u in range(modes):
         out_ref[u] = result[:, u * own_rows : (u + 1) * own_rows]
-    for started in asks + hands + ones + twos + sums + [last for step, last in lasts]:
+    for started in [swap] + asks + hands + ones + sums + [last for step, last in lasts]:
         started.wait_send()
+    others(early, lambda *way: second(*way).wait_send())
+    others(1 - early, lambda *way: second(*way).wait_send())
 
 
 def by_kernel(basis, ritz, phonon_g, band_index, qshift):
@@ -435,9 +472,10 @@
             pltpu.VMEM((count_exc, count_trans), jnp.float32),
             pltpu.VMEM((count_exc, count_trans), bf16),
             pltpu.VMEM((planes, 2, rows_cut // 2, LANES), bf16),
-            pltpu.VMEM((planes, 2, rows_cut // 2, LANES), bf16),
-            pltpu.VMEM((planes, 2, rows_cut // 2, LANES), bf16),
-            pltpu.VMEM((planes, 2, rows_cut // 2, LANES), bf16),
+            pltpu.VMEM((planes, rows_cut // 2, LANES), bf16),
+            pltpu.VMEM((2, planes, rows_cut // 2, LANES), bf16),
+            pltpu.VMEM((2, planes, rows_cut // 2, LANES), bf16),
+            pltpu.VMEM((2, 8, LANES), jnp.int32),
             pltpu.VMEM((planes_z, modes, own, count_trans), bf16),
             pltpu.VMEM((2, count_exc // 2, count_trans), bf16),
             pltpu.VMEM((2 * (planes_z - 1), count_exc // 2, modes * own), bf16),
@@ -446,14 +484,15 @@
             pltpu.VMEM((planes_x - 1, out_rows, modes * own), bf16),
             pltpu.VMEM((planes_x - 1, out_rows, modes * own), bf16),
             dma((5,)),
+            dma((2,)),
             dma((planes_x - 1,)),
             dma((planes_x - 1,)),
             dma((planes_x - 1,)),
             dma((planes_x - 1,)),
             dma((planes - 1,)),
             dma((planes - 1,)),
-            dma((2 * (planes - 1),)),
-            dma((2 * (planes - 1),)),
+            dma((2 * planes,)),
+            dma((2 * planes,)),
             dma((2 * (planes_z - 1),)),
             dma((2 * (planes_z - 1),)),
             dma((planes_x - 1,)),
@@ -480,6 +519,7 @@
     whole_tiles = (
         basis.shape[3] == NV * NC * LANES // 2
         and lax.axis_size("ex") == 2
+        and lax.axis_size("grp") == 2
         and planes % tiles == 0
         and planes_x * tiles == 2 * planes
         and count_exc % (planes // tiles * 32) == 0

time: 46.6 us -> 43.6 us (0.936)
  Pallas kernels: 44.6 us -> 41.8 us
    pallas_call x1, Pallas kernels: 44.6 us -> 41.8 us  [by_kernel(): pl.pallas_call(functools.partial(whole_step, planes_x, planes_z, norm_fac...]
where the time goes in v4:
time: 43.6 us; the launch traced here: 43.4 us
  Pallas kernels  41.8 us (96%)
  local copies, waits for them, and re-layouts  1.58 us (4%)
    pallas_call x1, Pallas kernels, by_kernel(): pl.pallas_call(functools.partial(whole_step, planes_x, planes_z, norm_fac...  41.8 us
    unnamed x1, local copies, waits for them, and re-layouts  1.58 us

profile of v4, /device:TPU:1, one launch (start us, length us, event | category | flops | bytes accessed | tf_op | source)
XLA Modules:
  0.0 43.4 jit_solution(9353525178606959633)
XLA Ops:
  0.0 41.8 %shard_map.55 = f32[6,48,48]{2,1,0:T(8,128)} custom-call(s32[8]{0:T(128)} %band_hbm.1, s32[3]{0:T(128)} %q_hbm.1, bf16[192,256]{1,0:T(8,128)(2,1)} %bitcast.5, bf16[6,16384]{1,0:T(8,128)(2,1)} %bitcast.4, bf16[1024,1024]{1,0:T(8,128)(2,1)} %bitcast.3), custom_call_target="tpu_custom_call" | custom-call | tf_op jit(solution)/shard_map/pallas_call | solution.py:459
  41.8 1.6 %copy.7 = f32[6,48,48]{2,1,0:T(8,128)} copy(f32[6,48,48]{2,1,0:T(8,128)} %shard_map.55) | data formatting | bytes 110592
